TPU v7x, 32 devices: a whole 2x2x4 slice. The times are simulated.
32 devices in a mesh: outer: 4 (over y, x), inner: 2 (over core), col: 4 (over z).
Axes of the slice: x: 2, y: 2, z: 4, core: 2. Of those that a mesh axis runs over, the one named last changes fastest.
Arguments:
- operator: bfloat16 [4096, 8192], P(('outer', 'inner'), 'col'), as said below
- test_matrix: bfloat16 [8192, 256], P('col'), may hold values from -6 to 6
Outputs:
- basis: float32 [4096, 256], P(('outer', 'inner'), 'col')
- factor: float32 [256, 256], replicated
Inputs may be any that keep to these rules, and one draw needn't show every extreme that they name: Entries of the operator are of order 1 / sqrt(8192) times row and column scales between 0.5 and 4.
All inputs are finite; a program needn't handle non-finite values.
Results may differ from a plain program's by a relative error of at most 0.003.
Values may be sent and summed in bfloat16 or wider, within the bound.
A program may use at most 64 MiB of HBM per device.

v0:
```python
import jax
import jax.numpy as jnp
from jax import lax
from jax.sharding import PartitionSpec as P


def right_solve(lower, matrix):
    return jax.scipy.linalg.solve_triangular(lower, matrix.T, lower=True).T


def transposed_product(block, sketch):
    return lax.dot_general(
        block, sketch, (((0,), (0,)), ((), ())), preferred_element_type=jnp.float32
    )


def shards(operator, test_matrix):
    row_groups = lax.axis_size("outer") * lax.axis_size("inner")
    col_groups = lax.axis_size("col")
    local_cols = operator.shape[1]
    total_rows = operator.shape[0] * row_groups
    total_cols = local_cols * col_groups
    ratio = total_cols / total_rows
    partial_sketch = jnp.dot(operator, test_matrix, preferred_element_type=jnp.float32)
    sketch = lax.psum(partial_sketch, "col").astype(jnp.bfloat16)
    partial_normal = transposed_product(operator, sketch)
    summed = lax.psum(partial_normal, ("outer", "inner"))
    normal = (summed * ratio).astype(jnp.bfloat16)
    partial_image = jnp.dot(operator, normal, preferred_element_type=jnp.float32)
    image = lax.psum(partial_image, "col")
    local_gram = jnp.dot(
        image.T, image, precision=lax.Precision.HIGHEST, preferred_element_type=jnp.float32
    )
    gram = lax.psum(local_gram, ("outer", "inner"))
    lower = jnp.linalg.cholesky(gram)
    width = image.shape[1] // col_groups
    orthonormal = right_solve(lower, image)
    root = jnp.sqrt(jnp.float32(total_rows))
    basis = lax.dynamic_slice_in_dim(orthonormal, lax.axis_index("col") * width, width, 1) * root
    factor = lower.T / root
    return (basis, factor)


def solution(mesh):
    placed = (P(("outer", "inner"), "col"), P("col", None))
    return jax.shard_map(
        shards,
        mesh=mesh,
        in_specs=placed,
        out_specs=(P(("outer", "inner"), "col"), P()),
        check_vma=False,
    )
```

profile of v0, /device:TPU:9, one launch (start us, length us, event | category | flops | bytes accessed | tf_op | source)
XLA Modules:
  0.0 273.5 jit_solution(421812006087493749)
XLA Ops:
  7.2 1.5 copy-done
  8.8 1.9 fusion.16
  10.7 23.2 %all-reduce.11 = bf16[512,256]{1,0:T(8,128)(2,1)S(1)} all-reduce(f32[512,256]{1,0:T(8,128)S(1)} %fusion.16), channel_id=1, replica_groups=mesh['outer'=4,'inner'=2,'col'=4] {'col'}, use_global_device_ids=true, to_apply=%region_0.0 | all-reduce | flops 131072 | bytes 786432 | tf_op jit(solution)/shard_map/psum | solution.py:25
  33.9 2.0 convolution_bitcast_fusion
  36.0 66.4 %all-reduce.6.cloned.1.call-done = f32[2048,256]{0,1:T(8,128)} async-done(((f32[2048,256]{0,1:T(8,128)}), f32[2048,256]{0,1:T(8,128)}) %all-reduce.6.cloned.1.call-update) | async-done | bytes 2097168 | tf_op jit(solution)/shard_map/psum | solution.py:27
  102.4 3.1 %convolution_bitcast_fusion.1 = f32[512,256]{0,1:T(8,128)} fusion(bf16[512,2048]{1,0:T(8,128)(2,1)S(1)} %copy-done, f32[2048,256]{0,1:T(8,128)} %all-reduce.6.cloned.1.call-done), kind=kOutput, calls=%fused_computation.4 | convolution fusion | flops 537919488 | bytes 4718592 | tf_op jit(solution)/shard_map/dot_general | solution.py:29
  105.8 37.2 %all-reduce.8.cloned.1.call-done = f32[512,256]{0,1:T(8,128)} async-done(((f32[512,256]{0,1:T(8,128)}), f32[512,256]{0,1:T(8,128)}) %all-reduce.8.cloned.1.call-update) | async-done | bytes 524304 | tf_op jit(solution)/shard_map/psum | solution.py:30
  143.0 2.5 fusion.17
  145.6 55.1 %all-reduce.10.cloned.1.call-done = f32[256,256]{0,1:T(8,128)} async-done(((f32[256,256]{0,1:T(8,128)}), f32[256,256]{0,1:T(8,128)}) %all-reduce.10.cloned.1.call-update) | async-done | bytes 262160 | tf_op jit(solution)/shard_map/psum | solution.py:34
  200.6 1.1 copy.5
  201.7 1.0 fusion.3
  202.7 11.7 %cholesky.50 = f32[128,128]{1,0:T(8,128)S(1)} custom-call(f32[128,128]{1,0:T(8,128)S(1)} %cholesky.118), custom_call_target="Cholesky" | custom-call | tf_op jit(solution)/shard_map/jit(cholesky)/cholesky | solution.py:35
  214.5 9.8 %custom-call.15 = f32[1,128,128]{1,2,0:T(8,128)S(1)} custom-call(f32[1,128,128]{2,1,0:T(8,128)S(1)} %get-tuple-element.27), custom_call_target="InvertDiagBlocksLowerTriangular" | custom-call | tf_op jit(solution)/shard_map/jit(cholesky)/cholesky | solution.py:35
  224.8 11.7 %cholesky.105 = f32[128,128]{1,0:T(8,128)S(1)} custom-call(f32[128,128]{1,0:T(8,128)S(1)} %convolution_subtract_fusion.1), custom_call_target="Cholesky" | custom-call | tf_op jit(solution)/shard_map/jit(cholesky)/cholesky | solution.py:35
  236.5 0.7 compare_reduce_fusion
  238.7 4.3 %while.1 = (s32[]{:T(128)}, f32[256,256]{1,0:T(8,128)S(1)}, s32[2,2]{1,0:T(2,128)S(1)}, f32[2,128,128]{2,1,0:T(8,128)S(1)}, s32[]{:T(128)}) while((s32[]{:T(128)}, f32[256,256]{1,0:T(8,128)S(1)}, s32[2,2]{1,0:T(2,128)S(1)}, f32[2,128,128]{2,1,0:T(8,128)S(1)}, s32[]{:T(128)}) %tuple.29), condition=%wide.while_cond, body=%wide.while_body.sunk | while | flops 2 | bytes 131181 | solution.py:8
  238.9 0.6 fusion.30
  239.5 1.4 bitcast_dynamic-update-slice_fusion.2
  241.0 0.6 fusion.30
  241.6 1.4 bitcast_dynamic-update-slice_fusion.2
  243.0 0.6 copy-done.2
  243.7 20.5 %custom-call.16 = f32[2,128,128]{1,2,0:T(8,128)S(1)} custom-call(f32[2,128,128]{2,1,0:T(8,128)} %copy-done.2), custom_call_target="InvertDiagBlocksLowerTriangular" | custom-call | tf_op jit(solution)/shard_map/jit(_solve_triangular)/triangular_solve | solution.py:8
  265.4 0.8 copy.6
  266.3 0.7 fusion.8
  (25 shorter events, 2.3 us)
Async XLA Ops:
  7.2 1.6 copy-start
  7.2 95.2 %all-reduce.6.cloned.1.call-start = ((), (), s32[]{:S(2)}) async-start(), calls=%async_computation | async-start | bytes 4194304 | tf_op jit(solution)/shard_map/psum | solution.py:27
  35.9 107.1 %all-reduce.8.cloned.1.call-start = ((), (), s32[]{:S(2)}) async-start(), calls=%async_computation.1 | async-start | bytes 1048576 | tf_op jit(solution)/shard_map/psum | solution.py:30
  105.6 95.1 %all-reduce.10.cloned.1.call-start = ((), (), s32[]{:S(2)}) async-start(), calls=%async_computation.2 | async-start | bytes 524288 | tf_op jit(solution)/shard_map/psum | solution.py:34
  145.5 118.6 %copy-start.1 = (f32[512,256]{0,1:T(8,128)S(1)}, f32[512,256]{0,1:T(8,128)}, u32[]{:S(2)}) copy-start(f32[512,256]{0,1:T(8,128)} %all-reduce.8.cloned.1.call-done) | copy-start | bytes 1572868
  243.0 0.7 copy-start.2
Sparse Core Ops, SparseCore 0:
  36.0 66.3 all-reduce.5
  105.7 37.2 all-reduce.7
  146.6 53.9 all-reduce.9
where the time goes:
time: 276 us; the launch traced here: 273 us
  waiting for transfers between devices  159 us (58%)
  other arithmetic  56.2 us (20%)
  blocking collectives  23.2 us (8%)
  between operations  15.2 us (6%)
  matrix products  11.3 us (4%)
  local copies, waits for them, and re-layouts  8.27 us (3%)
    psum x1, waiting for transfers between devices, shards(): summed = lax.psum(partial_normal, ('outer', 'inner'))  66.4 us
    psum x1, waiting for transfers between devices, shards(): gram = lax.psum(local_gram, ('outer', 'inner'))  55.1 us
    psum x1, waiting for transfers between devices, shards(): image = lax.psum(partial_image, 'col')  37.2 us
    another operation x6, other arithmetic, shards(): lower = jnp.linalg.cholesky(gram)  34 us
    psum x1, blocking collectives, shards(): sketch = lax.psum(partial_sketch, 'col').astype(jnp.bfloat16)  23.2 us
    another operation x2, other arithmetic, right_solve(): return jax.scipy.linalg.solve_triangular(lower, matrix.T, lower=True).T  20.5 us
  transfers between devices with their start and end apart: 3, of which 3 were waited for; matrix products, arithmetic and copies ran while one was open for 0% of the time, Pallas kernels for 0%

commit v1 on v0

v1 whole, which is shorter than its diff:
```python
import functools

import jax
import jax.numpy as jnp
from jax import lax
from jax.experimental import pallas as pl
from jax.experimental.pallas import tpu as pltpu
from jax.sharding import PartitionSpec as P

F32 = jnp.float32
BF16 = jnp.bfloat16
MESH = pl.DeviceIdType.MESH
HIGHEST = lax.Precision.HIGHEST
SKETCH_WIRE = F32
NORMAL_WIRE = F32
IMAGE_WIRE = F32


def power_kernel(
    sizes, ratio, a_hbm, om_hbm, gram_ref, image_ref,
    a, om, p1, w1, r1, sk, p2, w2, r2, nt, p3, w3, r3, x, gp, ra, gb, gf, im,
    load_sem, s0, v0, s1, v1, s2, v2, s3, v3, s4, v4, s5, v5, s6, v6, s7, v7, s8, v8, s9, v9,
):
    outer, inner, cols = sizes
    chips = inner // 2
    groups = outer * chips
    o, i, c = lax.axis_index("outer"), lax.axis_index("inner"), lax.axis_index("col")
    k = lax.rem(i, 2)
    other = 1 - k
    chip = lax.div(i, 2)
    r = o * chips + chip
    partner = (o, chip * 2 + other, c)

    def col_peer(s):
        return lax.rem(c + s, cols)

    def row_peer(s):
        return lax.rem(r + s, groups)

    def at_col(to, core):
        return (o, chip * 2 + core, to)

    def at_row(to):
        return (lax.div(to, chips), lax.rem(to, chips) * 2 + k, c)

    def send(src, dst, ss, rs, to):
        copy = pltpu.make_async_remote_copy(
            src_ref=src, dst_ref=dst, send_sem=ss, recv_sem=rs, device_id=to, device_id_type=MESH
        )
        copy.start()
        return copy

    load_a = pltpu.make_async_copy(a_hbm, a.at[k], load_sem.at[0])
    load_a.start()
    width = om.shape[1]
    load_om = pltpu.make_async_copy(
        om_hbm.at[:, pl.ds(pl.multiple_of(k * width, width), width)], om, load_sem.at[1]
    )
    load_om.start()

    barrier = pltpu.get_barrier_semaphore()
    peers = [partner]
    for s in range(1, cols):
        peers += [at_col(col_peer(s), k), at_col(col_peer(s), other)]
    for s in range(1, groups):
        peers.append(at_row(row_peer(s)))
    for to in peers:
        pl.semaphore_signal(barrier, inc=1, device_id=to, device_id_type=MESH)
    pl.semaphore_wait(barrier, len(peers))

    pair = send(a_hbm, a.at[k], s0, v0, partner)
    load_a.wait()
    load_om.wait()

    part = p1.shape[1] // cols
    own = pl.ds(pl.multiple_of(c * part, part), part)

    def rows_of(to):
        return pl.ds(pl.multiple_of(to * part, part), part)

    copies = []
    for turn, block in enumerate((k, other)):
        if turn == 1:
            pair.wait()
        partial = jnp.dot(a[block], om[...], preferred_element_type=F32)
        p1[block] = partial
        if SKETCH_WIRE != F32:
            w1[block] = partial.astype(SKETCH_WIRE)
        for s in range(1, cols):
            to = col_peer(s)
            n = (s - 1) * 2 + turn
            copies.append(send(
                (p1 if SKETCH_WIRE == F32 else w1).at[block, rows_of(to)],
                r1.at[s - 1, turn], s1.at[n], v1.at[n], at_col(to, k)))
    for copy in copies:
        copy.wait()
    for turn, block in enumerate((k, other)):
        total = p1[block, own]
        for s in range(1, cols):
            total = total + r1[s - 1, turn].astype(F32)
        sk[block, own] = total.astype(BF16)
    copies = []
    for s in range(1, cols):
        copies.append(send(sk.at[:, own], sk.at[:, own], s2.at[s - 1], v2.at[s - 1], at_col(col_peer(s), k)))
    for copy in copies:
        copy.wait()

    normal = None
    for block in range(2):
        st = sk[block].astype(F32).T.astype(BF16)
        term = jnp.dot(st, a[block], preferred_element_type=F32)
        normal = term if normal is None else normal + term
    lanes = p2.shape[1]
    for g in range(groups):
        p2[g] = normal[g * lanes:(g + 1) * lanes]
        if NORMAL_WIRE != F32:
            w2[g] = normal[g * lanes:(g + 1) * lanes].astype(NORMAL_WIRE)
    copies = []
    for s in range(1, groups):
        to = row_peer(s)
        copies.append(send((p2 if NORMAL_WIRE == F32 else w2).at[to], r2.at[s - 1], s3.at[s - 1], v3.at[s - 1], at_row(to)))
    for copy in copies:
        copy.wait()
    total = p2[r]
    for s in range(1, groups):
        total = total + r2[s - 1].astype(F32)
    nt[r] = (total * ratio).astype(BF16)
    copies = []
    for s in range(1, groups):
        copies.append(send(nt.at[r], nt.at[r], s4.at[s - 1], v4.at[s - 1], at_row(row_peer(s))))
    for copy in copies:
        copy.wait()
    if lanes % 16 == 0:
        whole = nt[...].reshape(groups * lanes, nt.shape[2])
    else:
        whole = jnp.concatenate([nt[g].astype(F32) for g in range(groups)], axis=0).astype(BF16)

    copies = []
    for block in range(2):
        partial = lax.dot_general(a[block], whole, (((1,), (1,)), ((), ())), preferred_element_type=F32)
        p3[block] = partial
        if IMAGE_WIRE != F32:
            w3[block] = partial.astype(IMAGE_WIRE)
        for s in range(1, cols):
            to = col_peer(s)
            n = (s - 1) * 2 + block
            copies.append(send(
                (p3 if IMAGE_WIRE == F32 else w3).at[block, rows_of(to)],
                r3.at[s - 1, block], s5.at[n], v5.at[n], at_col(to, k)))
    for copy in copies:
        copy.wait()
    for block in range(2):
        total = p3[block, own]
        for s in range(1, cols):
            total = total + r3[s - 1, block].astype(F32)
        x[k, block] = total
    pair = send(x.at[k], x.at[k], s6, v6, partner)
    pair.wait()
    im[c, k] = x[k, k]
    im[c, other] = x[other, k]

    mine = x[k].reshape(2 * part, width)
    grams = [
        lax.dot_general(x[j].reshape(2 * part, width), mine, (((0,), (0,)), ((), ())),
                        precision=HIGHEST, preferred_element_type=F32)
        for j in range(2)
    ]
    full = jnp.concatenate(grams, axis=0)
    piece = gp.shape[1]
    for to in range(cols):
        gp[to] = full[to * piece:(to + 1) * piece]
    copies = []
    for s in range(1, cols):
        to = col_peer(s)
        copies.append(send(gp.at[to], ra.at[s - 1], s7.at[s - 1], v7.at[s - 1], at_col(to, k)))
    images = []
    for s in range(1, cols):
        to = col_peer(s)
        images.append(send(x.at[k, k], im.at[c, k], s8.at[2 * s - 2], v8.at[2 * s - 2], at_col(to, k)))
        images.append(send(x.at[k, other], im.at[c, k], s8.at[2 * s - 1], v8.at[2 * s - 1], at_col(to, other)))
    for copy in copies:
        copy.wait()
    total = gp[c]
    for s in range(1, cols):
        total = total + ra[s - 1]
    gb[r] = total
    copies = []
    for s in range(1, groups):
        copies.append(send(gb.at[r], gb.at[r], s9.at[s - 1], v9.at[s - 1], at_row(row_peer(s))))
    for copy in copies:
        copy.wait()
    total = gb[0]
    for g in range(1, groups):
        total = total + gb[g]
    gf[k, c] = total
    copies = [send(gf.at[k, c], gf.at[k, c], load_sem.at[2], load_sem.at[3], partner)]
    n = 4
    for s in range(1, cols):
        for core in (k, other):
            copies.append(send(gf.at[k, c], gf.at[k, c], load_sem.at[n], load_sem.at[n + 1], at_col(col_peer(s), core)))
            n += 2
    for copy in copies:
        copy.wait()
    for copy in images:
        copy.wait()
    for core in range(2):
        for to in range(cols):
            gram_ref[to * piece:(to + 1) * piece, core * width:(core + 1) * width] = gf[core, to]
    for core in range(2):
        for to in range(cols):
            image_ref[to * part:(to + 1) * part, core * width:(core + 1) * width] = im[to, core]


def power_step(operator, test_matrix, sizes, ratio):
    outer, inner, cols = sizes
    rows, depth = operator.shape
    rank = test_matrix.shape[1]
    half = rank // 2
    groups = outer * inner // 2
    part = rows // cols
    lanes = half // groups
    dma = pltpu.SemaphoreType.DMA
    vmem = pltpu.VMEM
    blocks = (cols - 1, 2, part, half)
    tiny = (1, 8, 128)
    scratch = [
        vmem((2, rows, depth), BF16),
        vmem((depth, half), BF16),
        vmem((2, rows, half), F32),
        vmem((2, rows, half) if SKETCH_WIRE != F32 else tiny, SKETCH_WIRE),
        vmem(blocks, SKETCH_WIRE),
        vmem((2, rows, half), BF16),
        vmem((groups, lanes, depth), F32),
        vmem((groups, lanes, depth) if NORMAL_WIRE != F32 else tiny, NORMAL_WIRE),
        vmem((groups - 1, lanes, depth), NORMAL_WIRE),
        vmem((groups, lanes, depth), BF16),
        vmem((2, rows, half), F32),
        vmem((2, rows, half) if IMAGE_WIRE != F32 else tiny, IMAGE_WIRE),
        vmem(blocks, IMAGE_WIRE),
        vmem((2, 2, part, half), F32),
        vmem((cols, rank // cols, half), F32),
        vmem((cols - 1, rank // cols, half), F32),
        vmem((groups, rank // cols, half), F32),
        vmem((2, cols, rank // cols, half), F32),
        vmem((cols, 2, part, half), F32),
        dma((4 + 4 * (cols - 1),)),
        dma, dma,
    ]
    for count in (2 * (cols - 1), cols - 1, groups - 1, groups - 1, 2 * (cols - 1)):
        scratch += [dma((count,)), dma((count,))]
    scratch += [dma, dma]
    for count in (cols - 1, 2 * (cols - 1), groups - 1):
        scratch += [dma((count,)), dma((count,))]
    return pl.pallas_call(
        functools.partial(power_kernel, sizes, ratio),
        out_shape=(
            jax.ShapeDtypeStruct((rank, rank), F32),
            jax.ShapeDtypeStruct((rows, rank), F32),
        ),
        in_specs=[pl.BlockSpec(memory_space=pl.ANY)] * 2,
        out_specs=(pl.BlockSpec(memory_space=pltpu.VMEM),) * 2,
        scratch_shapes=scratch,
        compiler_params=pltpu.CompilerParams(
            collective_id=0, has_side_effects=True, vmem_limit_bytes=48 << 20
        ),
        name="power_step",
    )(operator, test_matrix)


def shards(operator, test_matrix):
    sizes = tuple(lax.axis_size(name) for name in ("outer", "inner", "col"))
    row_groups = sizes[0] * sizes[1]
    col_groups = sizes[2]
    total_rows = operator.shape[0] * row_groups
    total_cols = operator.shape[1] * col_groups
    gram, image = power_step(operator, test_matrix, sizes, total_cols / total_rows)
    lower = jnp.linalg.cholesky(gram)
    root = jnp.sqrt(jnp.float32(total_rows))
    width = image.shape[1] // col_groups
    orthonormal = jax.scipy.linalg.solve_triangular(lower, image.T, lower=True).T
    basis = lax.dynamic_slice_in_dim(orthonormal, lax.axis_index("col") * width, width, 1) * root
    factor = lower.T / root
    return (basis, factor)


def solution(mesh):
    placed = (P(("outer", "inner"), "col"), P("col", None))
    return jax.shard_map(
        shards,
        mesh=mesh,
        in_specs=placed,
        out_specs=(P(("outer", "inner"), "col"), P()),
        check_vma=False,
    )
```

time: 276 us -> 147 us (0.53)
  waiting for transfers between devices: 159 us -> 0 us
  Pallas kernels: 0 us -> 79.8 us
  blocking collectives: 23.2 us -> 0 us
  between operations: 15.2 us -> 2.06 us
  matrix products: 11.3 us -> 1.89 us
    psum x3 -> x0, waiting for transfers between devices: 159 us -> none  [the longest x1 66.4 us: shards(): summed = lax.psum(partial_normal, ('outer', 'inner'))]
    pallas_call x0 -> x1, Pallas kernels: none -> 79.8 us  [power_step(): pl.pallas_call(functools.partial(power_kernel, sizes, ratio), out_shape=(...]
    psum x1 -> x0, blocking collectives: 23.2 us -> none  [shards(): sketch = lax.psum(partial_sketch, 'col').astype(jnp.bfloat16)]
    dot_general x4 -> x0, matrix products: 9.62 us -> none  [the longest x1 3.14 us: shards(): jnp.dot(operator, normal, preferred_element_type=jnp.float32)]
  transfers between devices with their start and end apart: 3 -> 0, of which waited for: 3 -> 0; matrix products, arithmetic and copies ran while one was open for 0% -> 0% of each run, Pallas kernels for 0% -> 0%
where the time goes in v1:
time: 147 us; the launch traced here: 146 us
  Pallas kernels  79.8 us (54%)
  other arithmetic  54.5 us (37%)
  local copies, waits for them, and re-layouts  7.93 us (5%)
  between operations  2.06 us (1%)
  matrix products  1.89 us (1%)
    pallas_call x1, Pallas kernels, power_step(): pl.pallas_call(functools.partial(power_kernel, sizes, ratio), out_shape=(...  79.8 us
    another operation x6, other arithmetic, shards(): lower = jnp.linalg.cholesky(gram)  34.1 us
    another operation x2, other arithmetic, shards(): jax.scipy.linalg.solve_triangular(lower, image.T, lower=True)  19.7 us
    another operation x6, local copies, waits for them, and re-layouts  4.06 us
    unnamed x5, local copies, waits for them, and re-layouts  3.64 us

profile of v1, /device:TPU:9, one launch (start us, length us, event | category | flops | bytes accessed | tf_op | source)
XLA Modules:
  0.0 146.2 jit_solution(2052346141572632902)
XLA Ops:
  0.6 0.0 copy-start
  0.6 1.6 %copy-done = bf16[512,2048]{1,0:T(8,128)(2,1)S(1)} copy-done((bf16[512,2048]{1,0:T(8,128)(2,1)S(1)}, bf16[512,2048]{1,0:T(8,128)(2,1)}, u32[]{:S(2)}) %copy-start) | copy-done | bytes 2097176
  2.2 0.0 copy-start.1
  2.2 1.2 copy-done.1
  3.4 79.8 %power_step.1 = (f32[256,256]{1,0:T(8,128)S(1)}, f32[512,256]{1,0:T(8,128)S(1)}) custom-call(bf16[512,2048]{1,0:T(8,128)(2,1)S(1)} %copy-done, bf16[2048,256]{1,0:T(8,128)(2,1)S(1)} %copy-done.1), custom_call_target="tpu_custom_call" | custom-call | tf_op jit(solution)/shard_map/power_step/pallas_call | solution.py:254
  83.2 0.1 copy.4
  83.4 11.7 %cholesky.50 = f32[128,128]{1,0:T(8,128)S(1)} custom-call(f32[128,128]{1,0:T(8,128)S(1)} %cholesky.118), custom_call_target="Cholesky" | custom-call | tf_op jit(solution)/shard_map/jit(cholesky)/cholesky | solution.py:277
  95.2 9.8 %custom-call.15 = f32[1,128,128]{1,2,0:T(8,128)S(1)} custom-call(f32[1,128,128]{2,1,0:T(8,128)S(1)} %get-tuple-element.31), custom_call_target="InvertDiagBlocksLowerTriangular" | custom-call | tf_op jit(solution)/shard_map/jit(cholesky)/cholesky | solution.py:277
  105.0 0.2 constant_dynamic-update-slice_fusion
  105.2 0.3 convolution_subtract_fusion.1
  105.5 11.9 %cholesky.105 = f32[128,128]{1,0:T(8,128)S(1)} custom-call(f32[128,128]{1,0:T(8,128)S(1)} %convolution_subtract_fusion.1), custom_call_target="Cholesky" | custom-call | tf_op jit(solution)/shard_map/jit(cholesky)/cholesky | solution.py:277
  117.4 0.6 compare_reduce_fusion
  119.4 0.1 triangular_solve.57
  119.5 4.1 %while.1 = (s32[]{:T(128)}, f32[256,256]{1,0:T(8,128)S(1)}, s32[2,2]{1,0:T(2,128)S(1)}, f32[2,128,128]{2,1,0:T(8,128)S(1)}, s32[]{:T(128)}) while((s32[]{:T(128)}, f32[256,256]{1,0:T(8,128)S(1)}, s32[2,2]{1,0:T(2,128)S(1)}, f32[2,128,128]{2,1,0:T(8,128)S(1)}, s32[]{:T(128)}) %tuple.29), condition=%wide.while_cond, body=%wide.while_body.sunk | while | flops 2 | bytes 131181 | solution.py:280
  119.5 0.6 fusion.18
  120.1 1.4 bitcast_dynamic-update-slice_fusion.2
  121.5 0.6 fusion.18
  122.1 1.4 bitcast_dynamic-update-slice_fusion.2
  123.6 19.7 %custom-call.16 = f32[2,128,128]{1,2,0:T(8,128)S(1)} custom-call(f32[2,128,128]{2,1,0:T(8,128)S(1)} %get-tuple-element.13), custom_call_target="InvertDiagBlocksLowerTriangular" | custom-call | tf_op jit(solution)/shard_map/jit(_solve_triangular)/triangular_solve | solution.py:280
  143.3 0.4 fusion
  143.7 0.6 convolution_subtract_fusion
  144.3 0.4 fusion.8
  144.7 0.7 fusion.6
  145.4 0.8 copy.5
  (10 shorter events, 0.2 us)
Async XLA Ops:
  0.6 1.6 %copy-start = (bf16[512,2048]{1,0:T(8,128)(2,1)S(1)}, bf16[512,2048]{1,0:T(8,128)(2,1)}, u32[]{:S(2)}) copy-start(bf16[512,2048]{1,0:T(8,128)(2,1)} %a_hbm.1) | copy-start | bytes 6291460
  2.2 1.2 copy-start.1

commit v2 on v1

--- a/solution.py
+++ b/solution.py
@@ -14,6 +14,7 @@
 SKETCH_WIRE = F32
 NORMAL_WIRE = F32
 IMAGE_WIRE = F32
+BLOCK = 32
 
 
 def power_kernel(
@@ -261,10 +262,93 @@
         out_specs=(pl.BlockSpec(memory_space=pltpu.VMEM),) * 2,
         scratch_shapes=scratch,
         compiler_params=pltpu.CompilerParams(
-            collective_id=0, has_side_effects=True, vmem_limit_bytes=48 << 20
+            collective_id=0, has_side_effects=True, vmem_limit_bytes=60 << 20
         ),
         name="power_step",
     )(operator, test_matrix)
+
+
+def split(value):
+    high = value.astype(BF16)
+    rest = value - high.astype(F32)
+    middle = rest.astype(BF16)
+    low = (rest - middle.astype(F32)).astype(BF16)
+    return high, middle, low
+
+
+def factor_kernel(root, gram_ref, image_ref, basis_ref, factor_ref, s_ref, w_ref):
+    size = gram_ref.shape[0]
+    s_ref[...] = gram_ref[...]
+    row = lax.broadcasted_iota(jnp.int32, (size, size), 0)
+    col = lax.broadcasted_iota(jnp.int32, (size, size), 1)
+    w_ref[...] = jnp.where(row == col, jnp.float32(1), jnp.float32(0))
+    sub = lax.broadcasted_iota(jnp.int32, (8, 128), 0)
+    wide = 128
+    for start in range(0, size, BLOCK):
+        rows = BLOCK // 8
+        tiles = [(s_ref, t) for t in range(start // wide, size // wide)]
+        tiles += [(w_ref, t) for t in range(0, start // wide + 1)]
+        q = [[ref[start + 8 * g:start + 8 * g + 8, t * wide:(t + 1) * wide] for ref, t in tiles]
+             for g in range(rows)]
+        for p in range(rows):
+            first = (start + 8 * p) % wide
+            cs = [[jnp.broadcast_to(q[g][0][:, first + n:first + n + 1], (8, wide)) for n in range(8)]
+                  for g in range(p, rows)]
+            pivots = jnp.zeros((8, wide), F32)
+            for n in range(8):
+                pivot = jnp.broadcast_to(cs[0][n][n:n + 1], (8, wide))
+                pivots = jnp.where(sub == n, pivot, pivots)
+                inverse = 1.0 / pivot
+                heads = {m: jnp.broadcast_to(cs[0][m][n:n + 1], (8, wide)) * inverse for m in range(n + 1, 8)}
+                bodies = [jnp.broadcast_to(tile[n:n + 1], (8, wide)) * inverse for tile in q[p]]
+                for g in range(p, rows):
+                    weight = cs[g - p][n]
+                    if g == p:
+                        weight = jnp.where(sub > n, weight, 0.0)
+                    for m in range(n + 1, 8):
+                        cs[g - p][m] = cs[g - p][m] - weight * heads[m]
+                    q[g] = [tile - weight * body for tile, body in zip(q[g], bodies)]
+            scale = lax.rsqrt(pivots)
+            q[p] = [tile * scale for tile in q[p]]
+        for g in range(rows):
+            for (ref, t), tile in zip(tiles, q[g]):
+                ref[start + 8 * g:start + 8 * g + 8, t * wide:(t + 1) * wide] = tile
+        done = start + BLOCK
+        if done < size:
+            block = jnp.concatenate([jnp.concatenate(q[g], axis=1) for g in range(rows)], axis=0)
+            h, m, l = split(block)
+            count = size // wide - start // wide
+            base = (start // wide) * wide
+            take = slice(done - base, count * wide) if (done - base) % wide == 0 else slice(0, count * wide)
+            skip = done - base - (take.start or 0)
+            left = jnp.concatenate([h, h, m, m, h, l], axis=0)[:, take]
+            right = jnp.concatenate([h, m, h, m, l, h], axis=0)
+            update = lax.dot_general(left, right, (((0,), (0,)), ((), ())), preferred_element_type=F32)[skip:]
+            for at, (ref, t) in enumerate(tiles):
+                lanes = slice(t * wide, (t + 1) * wide)
+                ref[done:, lanes] = ref[done:, lanes] - update[:, at * wide:(at + 1) * wide]
+    factor_ref[...] = jnp.where(row <= col, s_ref[...], 0.0) / root
+    width = basis_ref.shape[1]
+    mine = pl.ds(pl.multiple_of(lax.axis_index("col") * width, width), width)
+    basis_ref[...] = lax.dot_general(
+        image_ref[...], w_ref[mine, :], (((1,), (1,)), ((), ())),
+        precision=HIGHEST, preferred_element_type=F32) * root
+
+
+def factor_step(gram, image, root, width):
+    size = gram.shape[0]
+    vmem = pl.BlockSpec(memory_space=pltpu.VMEM)
+    return pl.pallas_call(
+        functools.partial(factor_kernel, root),
+        out_shape=(
+            jax.ShapeDtypeStruct((image.shape[0], width), F32),
+            jax.ShapeDtypeStruct(gram.shape, F32),
+        ),
+        in_specs=[vmem, vmem],
+        out_specs=(vmem, vmem),
+        scratch_shapes=[pltpu.VMEM((size, size), F32), pltpu.VMEM((size, size), F32)],
+        name="factor_step",
+    )(gram, image)
 
 
 def shards(operator, test_matrix):
@@ -274,12 +358,8 @@
     total_rows = operator.shape[0] * row_groups
     total_cols = operator.shape[1] * col_groups
     gram, image = power_step(operator, test_matrix, sizes, total_cols / total_rows)
-    lower = jnp.linalg.cholesky(gram)
-    root = jnp.sqrt(jnp.float32(total_rows))
-    width = image.shape[1] // col_groups
-    orthonormal = jax.scipy.linalg.solve_triangular(lower, image.T, lower=True).T
-    basis = lax.dynamic_slice_in_dim(orthonormal, lax.axis_index("col") * width, width, 1) * root
-    factor = lower.T / root
+    root = float(total_rows) ** 0.5
+    basis, factor = factor_step(gram, image, root, image.shape[1] // col_groups)
     return (basis, factor)
 
 

time: 147 us -> 94 us (0.64)
  other arithmetic: 54.5 us -> 0 us
  Pallas kernels: 79.8 us -> 90.7 us
  local copies, waits for them, and re-layouts: 7.93 us -> 1.72 us
  matrix products: 1.89 us -> 0 us
    another operation x8 -> x0, other arithmetic: 53.8 us -> none  [the longest x6 34.1 us: shards(): lower = jnp.linalg.cholesky(gram)]
    pallas_call x0 -> x1, Pallas kernels: none -> 9.98 us  [factor_step(): pl.pallas_call(functools.partial(factor_kernel, root), out_shape=(jax.Sha...]
    another operation x9 -> x0, local copies, waits for them, and re-layouts: 4.16 us -> none
    unnamed x5 -> x0, local copies, waits for them, and re-layouts: 3.64 us -> none
    another operation x5 -> x0, matrix products: 1.89 us -> none  [the longest x3 1.42 us: shards(): jax.scipy.linalg.solve_triangular(lower, image.T, lower=True)]
    pallas_call x1, local copies, waits for them, and re-layouts: 0.13 us -> 1.72 us  [factor_step(): pl.pallas_call(functools.partial(factor_kernel, root), out_shape=(jax.Sha...]
where the time goes in v2:
time: 94 us; the launch traced here: 93.1 us
  Pallas kernels  90.7 us (96%)
  local copies, waits for them, and re-layouts  1.72 us (2%)
    pallas_call x1, Pallas kernels, power_step(): pl.pallas_call(functools.partial(power_kernel, sizes, ratio), out_shape=(...  80.8 us
    pallas_call x1, Pallas kernels, factor_step(): pl.pallas_call(functools.partial(factor_kernel, root), out_shape=(jax.Sha...  9.98 us

profile of v2, /device:TPU:9, one launch (start us, length us, event | category | flops | bytes accessed | tf_op | source)
XLA Modules:
  0.0 93.1 jit_solution(1164636879658588320)
XLA Ops:
  0.6 80.8 %power_step.1 = (f32[256,256]{1,0:T(8,128)}, f32[512,256]{1,0:T(8,128)}) custom-call(bf16[512,2048]{1,0:T(8,128)(2,1)} %a_hbm.1, bf16[2048,256]{1,0:T(8,128)(2,1)} %om_hbm.1), custom_call_target="tpu_custom_call" | custom-call | tf_op jit(solution)/shard_map/power_step/pallas_call | solution.py:255
  81.4 10.0 %factor_step.1 = (f32[512,64]{1,0:T(8,128)}, f32[256,256]{1,0:T(8,128)}) custom-call(f32[256,256]{1,0:T(8,128)} %get-tuple-element.4.gram_ref, f32[512,256]{1,0:T(8,128)} %get-tuple-element.5.image_ref), custom_call_target="tpu_custom_call" | custom-call | tf_op jit(solution)/shard_map/factor_step/pallas_call | solution.py:341
  91.4 1.7 %copy.4 = f32[512,64]{0,1:T(8,128)} copy(f32[512,64]{1,0:T(8,128)} %get-tuple-element.6) | data formatting | bytes 262144 | tf_op jit(solution)/shard_map/factor_step/pallas_call | solution.py:341

commit v3 on v1

--- a/solution.py
+++ b/solution.py
@@ -12,13 +12,74 @@
 MESH = pl.DeviceIdType.MESH
 HIGHEST = lax.Precision.HIGHEST
 SKETCH_WIRE = F32
-NORMAL_WIRE = F32
-IMAGE_WIRE = F32
+NORMAL_WIRE = BF16
+IMAGE_WIRE = BF16
+BLOCK = 32
+
+
+def split(value):
+    high = value.astype(BF16)
+    rest = value - high.astype(F32)
+    middle = rest.astype(BF16)
+    low = (rest - middle.astype(F32)).astype(BF16)
+    return high, middle, low
+
+
+def eliminate(s_ref, w_ref):
+    size = s_ref.shape[0]
+    row = lax.broadcasted_iota(jnp.int32, (size, size), 0)
+    col = lax.broadcasted_iota(jnp.int32, (size, size), 1)
+    w_ref[...] = jnp.where(row == col, jnp.float32(1), jnp.float32(0))
+    sub = lax.broadcasted_iota(jnp.int32, (8, 128), 0)
+    wide = 128
+    for start in range(0, size, BLOCK):
+        rows = BLOCK // 8
+        tiles = [(s_ref, t) for t in range(start // wide, size // wide)]
+        tiles += [(w_ref, t) for t in range(0, start // wide + 1)]
+        q = [[ref[start + 8 * g:start + 8 * g + 8, t * wide:(t + 1) * wide] for ref, t in tiles]
+             for g in range(rows)]
+        for p in range(rows):
+            first = (start + 8 * p) % wide
+            cs = [[jnp.broadcast_to(q[g][0][:, first + n:first + n + 1], (8, wide)) for n in range(8)]
+                  for g in range(p, rows)]
+            pivots = jnp.zeros((8, wide), F32)
+            for n in range(8):
+                pivot = jnp.broadcast_to(cs[0][n][n:n + 1], (8, wide))
+                pivots = jnp.where(sub == n, pivot, pivots)
+                inverse = 1.0 / pivot
+                heads = {m: jnp.broadcast_to(cs[0][m][n:n + 1], (8, wide)) * inverse for m in range(n + 1, 8)}
+                bodies = [jnp.broadcast_to(tile[n:n + 1], (8, wide)) * inverse for tile in q[p]]
+                for g in range(p, rows):
+                    weight = cs[g - p][n]
+                    if g == p:
+                        weight = jnp.where(sub > n, weight, 0.0)
+                    for m in range(n + 1, 8):
+                        cs[g - p][m] = cs[g - p][m] - weight * heads[m]
+                    q[g] = [tile - weight * body for tile, body in zip(q[g], bodies)]
+            scale = lax.rsqrt(pivots)
+            q[p] = [tile * scale for tile in q[p]]
+        for g in range(rows):
+            for (ref, t), tile in zip(tiles, q[g]):
+                ref[start + 8 * g:start + 8 * g + 8, t * wide:(t + 1) * wide] = tile
+        done = start + BLOCK
+        if done < size:
+            block = jnp.concatenate([jnp.concatenate(q[g], axis=1) for g in range(rows)], axis=0)
+            h, m, l = split(block)
+            count = size // wide - start // wide
+            base = (start // wide) * wide
+            take = slice(done - base, count * wide) if (done - base) % wide == 0 else slice(0, count * wide)
+            skip = done - base - (take.start or 0)
+            left = jnp.concatenate([h, h, m, m, h, l], axis=0)[:, take]
+            right = jnp.concatenate([h, m, h, m, l, h], axis=0)
+            update = lax.dot_general(left, right, (((0,), (0,)), ((), ())), preferred_element_type=F32)[skip:]
+            for at, (ref, t) in enumerate(tiles):
+                lanes = slice(t * wide, (t + 1) * wide)
+                ref[done:, lanes] = ref[done:, lanes] - update[:, at * wide:(at + 1) * wide]
 
 
 def power_kernel(
-    sizes, ratio, a_hbm, om_hbm, gram_ref, image_ref,
-    a, om, p1, w1, r1, sk, p2, w2, r2, nt, p3, w3, r3, x, gp, ra, gb, gf, im,
+    sizes, ratio, root, a_hbm, om_hbm, basis_ref, factor_ref,
+    a, om, p1, w1, r1, sk, p2, w2, r2, nt, p3, w3, r3, x, gp, ra, gb, gf, im, s_ref, w_ref,
     load_sem, s0, v0, s1, v1, s2, v2, s3, v3, s4, v4, s5, v5, s6, v6, s7, v7, s8, v8, s9, v9,
 ):
     outer, inner, cols = sizes
@@ -40,8 +101,8 @@
     def at_col(to, core):
         return (o, chip * 2 + core, to)
 
-    def at_row(to):
-        return (lax.div(to, chips), lax.rem(to, chips) * 2 + k, c)
+    def at_row(to, core):
+        return (lax.div(to, chips), lax.rem(to, chips) * 2 + core, c)
 
     def send(src, dst, ss, rs, to):
         copy = pltpu.make_async_remote_copy(
@@ -63,7 +124,7 @@
     for s in range(1, cols):
         peers += [at_col(col_peer(s), k), at_col(col_peer(s), other)]
     for s in range(1, groups):
-        peers.append(at_row(row_peer(s)))
+        peers += [at_row(row_peer(s), k), at_row(row_peer(s), other)]
     for to in peers:
         pl.semaphore_signal(barrier, inc=1, device_id=to, device_id_type=MESH)
     pl.semaphore_wait(barrier, len(peers))
@@ -118,7 +179,7 @@
     copies = []
     for s in range(1, groups):
         to = row_peer(s)
-        copies.append(send((p2 if NORMAL_WIRE == F32 else w2).at[to], r2.at[s - 1], s3.at[s - 1], v3.at[s - 1], at_row(to)))
+        copies.append(send((p2 if NORMAL_WIRE == F32 else w2).at[to], r2.at[s - 1], s3.at[s - 1], v3.at[s - 1], at_row(to, k)))
     for copy in copies:
         copy.wait()
     total = p2[r]
@@ -127,7 +188,7 @@
     nt[r] = (total * ratio).astype(BF16)
     copies = []
     for s in range(1, groups):
-        copies.append(send(nt.at[r], nt.at[r], s4.at[s - 1], v4.at[s - 1], at_row(row_peer(s))))
+        copies.append(send(nt.at[r], nt.at[r], s4.at[s - 1], v4.at[s - 1], at_row(row_peer(s), k)))
     for copy in copies:
         copy.wait()
     if lanes % 16 == 0:
@@ -167,12 +228,21 @@
     ]
     full = jnp.concatenate(grams, axis=0)
     piece = gp.shape[1]
-    for to in range(cols):
+    for to in range(groups):
         gp[to] = full[to * piece:(to + 1) * piece]
     copies = []
+    for s in range(1, groups):
+        to = row_peer(s)
+        copies.append(send(gp.at[to], ra.at[s - 1], s7.at[s - 1], v7.at[s - 1], at_row(to, k)))
+    for copy in copies:
+        copy.wait()
+    total = gp[r]
+    for s in range(1, groups):
+        total = total + ra[s - 1]
+    gb[c] = total
+    copies = []
     for s in range(1, cols):
-        to = col_peer(s)
-        copies.append(send(gp.at[to], ra.at[s - 1], s7.at[s - 1], v7.at[s - 1], at_col(to, k)))
+        copies.append(send(gb.at[c], gb.at[c], s9.at[s - 1], v9.at[s - 1], at_col(col_peer(s), k)))
     images = []
     for s in range(1, cols):
         to = col_peer(s)
@@ -180,38 +250,41 @@
         images.append(send(x.at[k, other], im.at[c, k], s8.at[2 * s - 1], v8.at[2 * s - 1], at_col(to, other)))
     for copy in copies:
         copy.wait()
-    total = gp[c]
-    for s in range(1, cols):
-        total = total + ra[s - 1]
-    gb[r] = total
-    copies = []
-    for s in range(1, groups):
-        copies.append(send(gb.at[r], gb.at[r], s9.at[s - 1], v9.at[s - 1], at_row(row_peer(s))))
-    for copy in copies:
-        copy.wait()
     total = gb[0]
-    for g in range(1, groups):
-        total = total + gb[g]
-    gf[k, c] = total
-    copies = [send(gf.at[k, c], gf.at[k, c], load_sem.at[2], load_sem.at[3], partner)]
+    for to in range(1, cols):
+        total = total + gb[to]
+    gf[k, r] = total
+    copies = [send(gf.at[k, r], gf.at[k, r], load_sem.at[2], load_sem.at[3], partner)]
     n = 4
-    for s in range(1, cols):
+    for s in range(1, groups):
         for core in (k, other):
-            copies.append(send(gf.at[k, c], gf.at[k, c], load_sem.at[n], load_sem.at[n + 1], at_col(col_peer(s), core)))
+            copies.append(send(gf.at[k, r], gf.at[k, r], load_sem.at[n], load_sem.at[n + 1], at_row(row_peer(s), core)))
             n += 2
     for copy in copies:
         copy.wait()
+    for core in range(2):
+        for g in range(groups):
+            s_ref[g * piece:(g + 1) * piece, core * width:(core + 1) * width] = gf[core, g]
+    eliminate(s_ref, w_ref)
+    size = s_ref.shape[0]
+    row = lax.broadcasted_iota(jnp.int32, (size, size), 0)
+    col = lax.broadcasted_iota(jnp.int32, (size, size), 1)
+    factor_ref[...] = jnp.where(row <= col, s_ref[...], 0.0) / root
+    columns = basis_ref.shape[0]
+    inverse = w_ref[pl.ds(pl.multiple_of(c * columns, columns), columns), :]
     for copy in images:
         copy.wait()
-    for core in range(2):
-        for to in range(cols):
-            gram_ref[to * piece:(to + 1) * piece, core * width:(core + 1) * width] = gf[core, to]
-    for core in range(2):
-        for to in range(cols):
-            image_ref[to * part:(to + 1) * part, core * width:(core + 1) * width] = im[to, core]
-
-
-def power_step(operator, test_matrix, sizes, ratio):
+    for to in range(cols):
+        total = None
+        for core in range(2):
+            term = lax.dot_general(
+                inverse[:, core * width:(core + 1) * width], im[to, core], (((1,), (1,)), ((), ())),
+                precision=HIGHEST, preferred_element_type=F32)
+            total = term if total is None else total + term
+        basis_ref[:, to * part:(to + 1) * part] = total * root
+
+
+def power_step(operator, test_matrix, sizes, ratio, root):
     outer, inner, cols = sizes
     rows, depth = operator.shape
     rank = test_matrix.shape[1]
@@ -238,30 +311,32 @@
         vmem((2, rows, half) if IMAGE_WIRE != F32 else tiny, IMAGE_WIRE),
         vmem(blocks, IMAGE_WIRE),
         vmem((2, 2, part, half), F32),
-        vmem((cols, rank // cols, half), F32),
-        vmem((cols - 1, rank // cols, half), F32),
-        vmem((groups, rank // cols, half), F32),
-        vmem((2, cols, rank // cols, half), F32),
+        vmem((groups, rank // groups, half), F32),
+        vmem((groups - 1, rank // groups, half), F32),
+        vmem((cols, rank // groups, half), F32),
+        vmem((2, groups, rank // groups, half), F32),
         vmem((cols, 2, part, half), F32),
-        dma((4 + 4 * (cols - 1),)),
+        vmem((rank, rank), F32),
+        vmem((rank, rank), F32),
+        dma((4 + 4 * (groups - 1),)),
         dma, dma,
     ]
     for count in (2 * (cols - 1), cols - 1, groups - 1, groups - 1, 2 * (cols - 1)):
         scratch += [dma((count,)), dma((count,))]
     scratch += [dma, dma]
-    for count in (cols - 1, 2 * (cols - 1), groups - 1):
+    for count in (groups - 1, 2 * (cols - 1), cols - 1):
         scratch += [dma((count,)), dma((count,))]
     return pl.pallas_call(
-        functools.partial(power_kernel, sizes, ratio),
+        functools.partial(power_kernel, sizes, ratio, root),
         out_shape=(
+            jax.ShapeDtypeStruct((rank // cols, rows), F32),
             jax.ShapeDtypeStruct((rank, rank), F32),
-            jax.ShapeDtypeStruct((rows, rank), F32),
         ),
         in_specs=[pl.BlockSpec(memory_space=pl.ANY)] * 2,
         out_specs=(pl.BlockSpec(memory_space=pltpu.VMEM),) * 2,
         scratch_shapes=scratch,
         compiler_params=pltpu.CompilerParams(
-            collective_id=0, has_side_effects=True, vmem_limit_bytes=48 << 20
+            collective_id=0, has_side_effects=True, vmem_limit_bytes=60 << 20
         ),
         name="power_step",
     )(operator, test_matrix)
@@ -273,14 +348,9 @@
     col_groups = sizes[2]
     total_rows = operator.shape[0] * row_groups
     total_cols = operator.shape[1] * col_groups
-    gram, image = power_step(operator, test_matrix, sizes, total_cols / total_rows)
-    lower = jnp.linalg.cholesky(gram)
-    root = jnp.sqrt(jnp.float32(total_rows))
-    width = image.shape[1] // col_groups
-    orthonormal = jax.scipy.linalg.solve_triangular(lower, image.T, lower=True).T
-    basis = lax.dynamic_slice_in_dim(orthonormal, lax.axis_index("col") * width, width, 1) * root
-    factor = lower.T / root
-    return (basis, factor)
+    root = float(total_rows) ** 0.5
+    basis, factor = power_step(operator, test_matrix, sizes, total_cols / total_rows, root)
+    return (basis.T, factor)
 
 
 def solution(mesh):

time: 147 us -> 82.2 us (0.56)
  other arithmetic: 54.5 us -> 0 us
  local copies, waits for them, and re-layouts: 7.93 us -> 3.24 us
  Pallas kernels: 79.8 us -> 77.3 us
  matrix products: 1.89 us -> 0 us
    another operation x8 -> x0, other arithmetic: 53.8 us -> none  [the longest x6 34.1 us: shards(): lower = jnp.linalg.cholesky(gram)]
    another operation x9 -> x0, local copies, waits for them, and re-layouts: 4.16 us -> none
    pallas_call x1, Pallas kernels: 79.8 us -> 77.3 us  [power_step(): pl.pallas_call(functools.partial(power_kernel, sizes, ratio, root), out_s...]
    another operation x5 -> x0, matrix products: 1.89 us -> none  [the longest x3 1.42 us: shards(): jax.scipy.linalg.solve_triangular(lower, image.T, lower=True)]
    unnamed x5 -> x2, local copies, waits for them, and re-layouts: 3.64 us -> 3.24 us
where the time goes in v3:
time: 82.2 us; the launch traced here: 81.2 us
  Pallas kernels  77.3 us (94%)
  local copies, waits for them, and re-layouts  3.24 us (4%)
    pallas_call x1, Pallas kernels, power_step(): pl.pallas_call(functools.partial(power_kernel, sizes, ratio, root), out_s...  77.3 us
    unnamed x2, local copies, waits for them, and re-layouts  3.24 us

profile of v3, /device:TPU:9, one launch (start us, length us, event | category | flops | bytes accessed | tf_op | source)
XLA Modules:
  0.0 81.2 jit_solution(10541828303796826866)
XLA Ops:
  0.6 77.3 %power_step.1 = (f32[64,512]{1,0:T(8,128)}, f32[256,256]{1,0:T(8,128)}) custom-call(bf16[512,2048]{1,0:T(8,128)(2,1)} %a_hbm.1, bf16[2048,256]{1,0:T(8,128)(2,1)} %om_hbm.1), custom_call_target="tpu_custom_call" | custom-call | tf_op jit(solution)/shard_map/power_step/pallas_call | solution.py:329
  78.0 1.6 %copy.6 = f32[512,64]{0,1:T(8,128)} copy(f32[512,64]{0,1:T(8,128)} %bitcast.1) | data formatting | bytes 262144
  79.5 1.7 %copy.7 = f32[256,256]{1,0:T(8,128)} copy(f32[256,256]{1,0:T(8,128)} %get-tuple-element.9) | data formatting | bytes 524288

commit v4 on v3

--- a/solution.py
+++ b/solution.py
@@ -11,7 +11,7 @@
 BF16 = jnp.bfloat16
 MESH = pl.DeviceIdType.MESH
 HIGHEST = lax.Precision.HIGHEST
-SKETCH_WIRE = F32
+SPANS = 2
 NORMAL_WIRE = BF16
 IMAGE_WIRE = BF16
 BLOCK = 32
@@ -79,7 +79,7 @@
 
 def power_kernel(
     sizes, ratio, root, a_hbm, om_hbm, basis_ref, factor_ref,
-    a, om, p1, w1, r1, sk, p2, w2, r2, nt, p3, w3, r3, x, gp, ra, gb, gf, im, s_ref, w_ref,
+    a, om, p1, r1, sk, p2, w2, r2, nt, p3, w3, r3, x, gp, ra, gb, gf, im, s_ref, w_ref,
     load_sem, s0, v0, s1, v1, s2, v2, s3, v3, s4, v4, s5, v5, s6, v6, s7, v7, s8, v8, s9, v9,
 ):
     outer, inner, cols = sizes
@@ -127,11 +127,11 @@
         peers += [at_row(row_peer(s), k), at_row(row_peer(s), other)]
     for to in peers:
         pl.semaphore_signal(barrier, inc=1, device_id=to, device_id_type=MESH)
-    pl.semaphore_wait(barrier, len(peers))
-
-    pair = send(a_hbm, a.at[k], s0, v0, partner)
     load_a.wait()
     load_om.wait()
+    p1[k] = jnp.dot(a[k], om[...], preferred_element_type=F32)
+    pl.semaphore_wait(barrier, len(peers))
+    pair = send(a_hbm, a.at[k], s0, v0, partner)
 
     part = p1.shape[1] // cols
     own = pl.ds(pl.multiple_of(c * part, part), part)
@@ -139,74 +139,92 @@
     def rows_of(to):
         return pl.ds(pl.multiple_of(to * part, part), part)
 
-    copies = []
+    sums = []
     for turn, block in enumerate((k, other)):
         if turn == 1:
             pair.wait()
-        partial = jnp.dot(a[block], om[...], preferred_element_type=F32)
-        p1[block] = partial
-        if SKETCH_WIRE != F32:
-            w1[block] = partial.astype(SKETCH_WIRE)
+            p1[block] = jnp.dot(a[block], om[...], preferred_element_type=F32)
+        copies = []
         for s in range(1, cols):
             to = col_peer(s)
             n = (s - 1) * 2 + turn
-            copies.append(send(
-                (p1 if SKETCH_WIRE == F32 else w1).at[block, rows_of(to)],
-                r1.at[s - 1, turn], s1.at[n], v1.at[n], at_col(to, k)))
-    for copy in copies:
-        copy.wait()
+            copies.append(send(p1.at[block, rows_of(to)], r1.at[s - 1, turn], s1.at[n], v1.at[n], at_col(to, k)))
+        sums.append(copies)
+    wholes = []
     for turn, block in enumerate((k, other)):
+        for copy in sums[turn]:
+            copy.wait()
         total = p1[block, own]
         for s in range(1, cols):
             total = total + r1[s - 1, turn].astype(F32)
         sk[block, own] = total.astype(BF16)
+        copies = []
+        for s in range(1, cols):
+            n = (s - 1) * 2 + turn
+            copies.append(send(sk.at[block, own], sk.at[block, own], s2.at[n], v2.at[n], at_col(col_peer(s), k)))
+        wholes.append(copies)
+
+    turned = []
+    for turn, block in enumerate((k, other)):
+        for copy in wholes[turn]:
+            copy.wait()
+        turned.append(sk[block].astype(F32).T.astype(BF16))
+    lanes = p2.shape[2]
+    depth = p2.shape[3]
+    sums = []
+    for span in range(SPANS):
+        at = slice(span * depth, (span + 1) * depth)
+        normal = None
+        for st, block in zip(turned, (k, other)):
+            term = jnp.dot(st, a[block, :, at], preferred_element_type=F32)
+            normal = term if normal is None else normal + term
+        for g in range(groups):
+            p2[span, g] = normal[g * lanes:(g + 1) * lanes]
+            w2[span, g] = normal[g * lanes:(g + 1) * lanes].astype(NORMAL_WIRE)
+        copies = []
+        for s in range(1, groups):
+            to = row_peer(s)
+            copies.append(send(w2.at[span, to], r2.at[span, s - 1], s3.at[span, s - 1], v3.at[span, s - 1], at_row(to, k)))
+        sums.append(copies)
+    wholes = []
+    for span in range(SPANS):
+        for copy in sums[span]:
+            copy.wait()
+        total = p2[span, r]
+        for s in range(1, groups):
+            total = total + r2[span, s - 1].astype(F32)
+        nt[span, r] = (total * ratio).astype(BF16)
+        copies = []
+        for s in range(1, groups):
+            copies.append(send(nt.at[span, r], nt.at[span, r], s4.at[span, s - 1], v4.at[span, s - 1], at_row(row_peer(s), k)))
+        wholes.append(copies)
+
     copies = []
-    for s in range(1, cols):
-        copies.append(send(sk.at[:, own], sk.at[:, own], s2.at[s - 1], v2.at[s - 1], at_col(col_peer(s), k)))
-    for copy in copies:
-        copy.wait()
-
-    normal = None
+    spans = []
+    for span in range(SPANS):
+        for copy in wholes[span]:
+            copy.wait()
+        if lanes % 16 == 0:
+            spans.append(nt[span].reshape(groups * lanes, depth))
+        else:
+            spans.append(jnp.concatenate([nt[span, g].astype(F32) for g in range(groups)], axis=0).astype(BF16))
+        if span < SPANS - 1:
+            for block in range(2):
+                term = lax.dot_general(a[block, :, span * depth:(span + 1) * depth], spans[span],
+                                       (((1,), (1,)), ((), ())), preferred_element_type=F32)
+                p3[block] = term if span == 0 else p3[block] + term
     for block in range(2):
-        st = sk[block].astype(F32).T.astype(BF16)
-        term = jnp.dot(st, a[block], preferred_element_type=F32)
-        normal = term if normal is None else normal + term
-    lanes = p2.shape[1]
-    for g in range(groups):
-        p2[g] = normal[g * lanes:(g + 1) * lanes]
-        if NORMAL_WIRE != F32:
-            w2[g] = normal[g * lanes:(g + 1) * lanes].astype(NORMAL_WIRE)
-    copies = []
-    for s in range(1, groups):
-        to = row_peer(s)
-        copies.append(send((p2 if NORMAL_WIRE == F32 else w2).at[to], r2.at[s - 1], s3.at[s - 1], v3.at[s - 1], at_row(to, k)))
-    for copy in copies:
-        copy.wait()
-    total = p2[r]
-    for s in range(1, groups):
-        total = total + r2[s - 1].astype(F32)
-    nt[r] = (total * ratio).astype(BF16)
-    copies = []
-    for s in range(1, groups):
-        copies.append(send(nt.at[r], nt.at[r], s4.at[s - 1], v4.at[s - 1], at_row(row_peer(s), k)))
-    for copy in copies:
-        copy.wait()
-    if lanes % 16 == 0:
-        whole = nt[...].reshape(groups * lanes, nt.shape[2])
-    else:
-        whole = jnp.concatenate([nt[g].astype(F32) for g in range(groups)], axis=0).astype(BF16)
-
-    copies = []
-    for block in range(2):
-        partial = lax.dot_general(a[block], whole, (((1,), (1,)), ((), ())), preferred_element_type=F32)
+        partial = lax.dot_general(a[block, :, (SPANS - 1) * depth:], spans[-1],
+                                  (((1,), (1,)), ((), ())), preferred_element_type=F32)
+        if SPANS > 1:
+            partial = p3[block] + partial
         p3[block] = partial
-        if IMAGE_WIRE != F32:
-            w3[block] = partial.astype(IMAGE_WIRE)
+        w3[block] = partial.astype(IMAGE_WIRE)
         for s in range(1, cols):
             to = col_peer(s)
             n = (s - 1) * 2 + block
             copies.append(send(
-                (p3 if IMAGE_WIRE == F32 else w3).at[block, rows_of(to)],
+                w3.at[block, rows_of(to)],
                 r3.at[s - 1, block], s5.at[n], v5.at[n], at_col(to, k)))
     for copy in copies:
         copy.wait()
@@ -295,20 +313,19 @@
     dma = pltpu.SemaphoreType.DMA
     vmem = pltpu.VMEM
     blocks = (cols - 1, 2, part, half)
-    tiny = (1, 8, 128)
+    span = depth // SPANS
     scratch = [
         vmem((2, rows, depth), BF16),
         vmem((depth, half), BF16),
         vmem((2, rows, half), F32),
-        vmem((2, rows, half) if SKETCH_WIRE != F32 else tiny, SKETCH_WIRE),
-        vmem(blocks, SKETCH_WIRE),
+        vmem(blocks, F32),
         vmem((2, rows, half), BF16),
-        vmem((groups, lanes, depth), F32),
-        vmem((groups, lanes, depth) if NORMAL_WIRE != F32 else tiny, NORMAL_WIRE),
-        vmem((groups - 1, lanes, depth), NORMAL_WIRE),
-        vmem((groups, lanes, depth), BF16),
+        vmem((SPANS, groups, lanes, span), F32),
+        vmem((SPANS, groups, lanes, span), NORMAL_WIRE),
+        vmem((SPANS, groups - 1, lanes, span), NORMAL_WIRE),
+        vmem((SPANS, groups, lanes, span), BF16),
         vmem((2, rows, half), F32),
-        vmem((2, rows, half) if IMAGE_WIRE != F32 else tiny, IMAGE_WIRE),
+        vmem((2, rows, half), IMAGE_WIRE),
         vmem(blocks, IMAGE_WIRE),
         vmem((2, 2, part, half), F32),
         vmem((groups, rank // groups, half), F32),
@@ -321,8 +338,9 @@
         dma((4 + 4 * (groups - 1),)),
         dma, dma,
     ]
-    for count in (2 * (cols - 1), cols - 1, groups - 1, groups - 1, 2 * (cols - 1)):
-        scratch += [dma((count,)), dma((count,))]
+    across, along = (2 * (cols - 1),), (SPANS, groups - 1)
+    for shape in (across, across, along, along, across):
+        scratch += [dma(shape), dma(shape)]
     scratch += [dma, dma]
     for count in (groups - 1, 2 * (cols - 1), cols - 1):
         scratch += [dma((count,)), dma((count,))]

time: 82.2 us -> 76.7 us (0.933)
  Pallas kernels: 77.3 us -> 72.6 us
    pallas_call x1, Pallas kernels: 77.3 us -> 72.6 us  [power_step(): pl.pallas_call(functools.partial(power_kernel, sizes, ratio, root), out_s...]
where the time goes in v4:
time: 76.7 us; the launch traced here: 76.5 us
  Pallas kernels  72.6 us (95%)
  local copies, waits for them, and re-layouts  3.24 us (4%)
    pallas_call x1, Pallas kernels, power_step(): pl.pallas_call(functools.partial(power_kernel, sizes, ratio, root), out_s...  72.6 us
    unnamed x2, local copies, waits for them, and re-layouts  3.24 us

profile of v4, /device:TPU:9, one launch (start us, length us, event | category | flops | bytes accessed | tf_op | source)
XLA Modules:
  0.0 76.5 jit_solution(11783803685931553623)
XLA Ops:
  0.6 72.6 %power_step.1 = (f32[64,512]{1,0:T(8,128)}, f32[256,256]{1,0:T(8,128)}) custom-call(bf16[512,2048]{1,0:T(8,128)(2,1)} %a_hbm.1, bf16[2048,256]{1,0:T(8,128)(2,1)} %om_hbm.1), custom_call_target="tpu_custom_call" | custom-call | tf_op jit(solution)/shard_map/power_step/pallas_call | solution.py:347
  73.3 1.6 %copy.6 = f32[512,64]{0,1:T(8,128)} copy(f32[512,64]{0,1:T(8,128)} %bitcast.1) | data formatting | bytes 262144
  74.8 1.7 %copy.7 = f32[256,256]{1,0:T(8,128)} copy(f32[256,256]{1,0:T(8,128)} %get-tuple-element.9) | data formatting | bytes 524288
